TPU v7x, 32 devices: a whole 2x2x4 slice. The times are simulated.
32 devices in a mesh: parts: 2 (over x), space: 16 (over z, y, core).
Axes of the slice: x: 2, y: 2, z: 4, core: 2. Of those that a mesh axis runs over, the one named last changes fastest.
Arguments:
- volume: bfloat16 [64, 16, 16, 128], P(('parts', 'space')), parts along dimension 0, may hold values from -6 to 6
- first_filter: bfloat16 [3, 3, 3, 128, 128], replicated, may hold values from -0.109375 to 0.109375
- second_filter: bfloat16 [3, 3, 3, 128, 128], replicated, may hold values from -0.109375 to 0.109375
- cotangent: bfloat16 [64, 16, 16, 128], P(('parts', 'space')), parts along dimension 0, may hold values from -0.06591797 to 0.06591797
Outputs:
- response: bfloat16 [64, 16, 16, 128], P(('parts', 'space')), parts along dimension 0
- first_grad: float32 [256, 3, 3, 3, 128], P(('parts', 'space')), parts along dimension 0
- second_grad: float32 [256, 3, 3, 3, 128], P(('parts', 'space')), parts along dimension 0
There are 2 independent parts, one for each index of `parts`. A program takes and returns all parts, laid end to end along the dimension named above; an argument that names none is the same for every part. Nothing has to cross between parts.
All inputs are finite; a program needn't handle non-finite values.
Results may differ from a plain program's by a relative error of at most 0.0049.
Values may be sent and summed in bfloat16 or wider, within the bound.
A program may use at most 64 MiB of HBM per device.

v0:
```python
import jax
import jax.numpy as jnp
from jax import lax
from jax.sharding import PartitionSpec as P


def padded_2(shard, sides, width):
    for axis, dim in sides:
        size, length = (lax.axis_size(axis), shard.shape[dim])
        up = [(i, (i + 1) % size) for i in range(size - 1)]
        down = [(j, i) for i, j in up]
        last = lax.slice_in_dim(shard, length - width, length, axis=dim)
        first = lax.slice_in_dim(shard, 0, width, axis=dim)
        before = lax.ppermute(last, axis, up)
        after = lax.ppermute(first, axis, down)
        shard = jnp.concatenate([before, shard, after], axis=dim)
    return shard


def spread(field):
    return jnp.pad(field, ((0, 0), (1, 1), (1, 1), (0, 0)))


def convolve(padded, weight):
    depth = padded.shape[0] - 2
    width = padded.shape[1] - 2
    height = padded.shape[2] - 2
    inner = padded.shape[3]
    total = jnp.zeros((depth * width * height, weight.shape[4]), jnp.float32)
    for plane in range(3):
        for column in range(3):
            slab = jnp.concatenate(
                [
                    padded[plane : plane + depth, column : column + width, lane : lane + height, :]
                    for lane in range(3)
                ],
                axis=-1,
            )
            total = total + jnp.dot(
                slab.reshape(-1, 3 * inner),
                weight[plane, column].reshape(3 * inner, -1),
                preferred_element_type=jnp.float32,
            )
    return total.reshape(depth, width, height, -1)


def weight_term(padded, grads, count):
    depth, width, height, outer = grads.shape
    flat = grads.reshape(-1, outer)
    blocks = []
    for plane in range(3):
        for column in range(3):
            slab = jnp.concatenate(
                [
                    padded[plane : plane + depth, column : column + width, lane : lane + height, :]
                    for lane in range(3)
                ],
                axis=-1,
            )
            term = lax.dot_general(
                slab.reshape(-1, 3 * count),
                flat,
                (((0,), (0,)), ((), ())),
                preferred_element_type=jnp.float32,
            )
            blocks.append(term.reshape(3, count, outer))
    stacked = jnp.stack(blocks, 0).reshape(3, 3, 3, count, outer)
    return jnp.transpose(stacked, (3, 0, 1, 2, 4))


def flipped(weight):
    return jnp.swapaxes(jnp.flip(weight, (0, 1, 2)), 3, 4)


def per_device(volume, first_filter, second_filter, cotangent):
    rim_in = padded_2(volume, (("space", 0),), 1)
    rim_cot = None
    padded_in = spread(rim_in)
    hidden = convolve(padded_in, first_filter)
    activated = jax.nn.silu(hidden).astype(jnp.bfloat16)
    padded_act = spread(padded_2(activated, (("space", 0),), 1))
    response = convolve(padded_act, second_filter).astype(jnp.bfloat16)
    rim_cot = padded_2(cotangent, (("space", 0),), 1)
    padded_cot = spread(rim_cot)
    act_grad = convolve(padded_cot, flipped(second_filter))
    sigma = jax.nn.sigmoid(hidden)
    hidden_grad = (act_grad * sigma * (1.0 + hidden * (1.0 - sigma))).astype(jnp.bfloat16)
    channels = volume.shape[3]
    second_local = weight_term(padded_act, cotangent, channels)
    first_local = weight_term(padded_in, hidden_grad, channels)
    second_grad = lax.psum_scatter(second_local, "space", scatter_dimension=0, tiled=True)
    first_grad = lax.psum_scatter(first_local, "space", scatter_dimension=0, tiled=True)
    return (response, first_grad, second_grad)


def solution(mesh):
    return jax.shard_map(
        per_device,
        mesh=mesh,
        in_specs=(
            P(("parts", "space"), None, None, None),
            P(),
            P(),
            P(("parts", "space"), None, None, None),
        ),
        out_specs=(
            P(("parts", "space"), None, None, None),
            P(("parts", "space"), None, None, None, None),
            P(("parts", "space"), None, None, None, None),
        ),
        check_vma=False,
    )
```

profile of v0, /device:TPU:0, one launch (start us, length us, event | category | flops | bytes accessed | tf_op | source)
XLA Modules:
  0.0 193.6 jit_solution(6003647268394256088)
XLA Ops:
  7.2 0.9 fusion.57
  8.1 2.4 %collective-permute-start = (bf16[1,16,16,128]{3,2,1,0:T(8,128)(2,1)S(1)}, bf16[1,16,16,128]{3,2,1,0:T(8,128)(2,1)S(1)}, u32[]{:S(2)}, u32[]{:S(2)}) collective-permute-start(bf16[1,16,16,128]{3,2,1,0:T(8,128)(2,1)S(1)} %get-tuple-element.115), channel_id=1, source_target_pairs={{0,1},{1,2},{2,3},{3,4},{4,5},{5,6},{6,7},{7,8},{8,9},{9,10},{10,1... | collective-permute-start | bytes 196616 | tf_op jit(solution)/shard_map/ppermute | solution.py:14
  10.5 1.3 collective-permute-start.1
  11.8 0.9 fusion.55
  12.7 5.2 %collective-permute-start.4 = (bf16[1,16,16,128]{3,2,1,0:T(8,128)(2,1)S(1)}, bf16[1,16,16,128]{3,2,1,0:T(8,128)(2,1)S(1)}, u32[]{:S(2)}, u32[]{:S(2)}) collective-permute-start(bf16[1,16,16,128]{3,2,1,0:T(8,128)(2,1)S(1)} %get-tuple-element.105), channel_id=1, source_target_pairs={{0,1},{1,2},{2,3},{3,4},{4,5},{5,6},{6,7},{7,8},{8,9},{9,10},{10,1... | collective-permute-start | bytes 196616 | tf_op jit(solution)/shard_map/ppermute | solution.py:14
  17.9 1.3 collective-permute-start.5
  19.2 2.0 %copy.26 = bf16[3,3,3,128,128]{3,4,2,1,0:T(8,128)(2,1)S(1)} copy(bf16[3,3,3,128,128]{4,3,2,1,0:T(8,128)(2,1)} %param.6) | data formatting | bytes 1769472 | tf_op args[2]
  21.3 1.0 fusion.46
  22.7 0.9 fusion.48
  23.8 1.4 fusion.49
  25.2 0.9 fusion.50
  26.3 0.8 fusion.54
  27.2 1.1 fusion.53
  28.4 0.9 copy.34
  29.4 1.0 copy.32
  30.4 0.9 copy.31
  31.4 1.0 copy.29
  32.4 0.9 copy.28
  33.3 2.3 %fusion.43 = (bf16[2,16,16,384]{3,2,1,0:T(8,128)(2,1)S(1)}, bf16[2,16,16,384]{3,2,1,0:T(8,128)(2,1)}, bf16[2,16,16,384]{3,2,1,0:T(8,128)(2,1)S(1)}, bf16[2,16,16,384]{3,2,1,0:T(8,128)(2,1)S(1)}) fusion(bf16[1,16,16,128]{3,2,1,0:T(8,128)(2,1)} %copy-done.71, bf16[2,16,16,128]{3,2,1,0:T(8,128)(2,1)S(1)} %copy-done.25, ...), kind=kLoop, calls=%fused_computation.99 | loop fusion | flops 5505024 | bytes 3014656 | tf_op jit(solution)/shard_map/concatenate | solution.py:32
  35.7 1.0 copy.25
  36.6 1.9 fusion.58
  38.5 0.9 copy.33
  39.4 0.9 copy.30
  40.4 1.0 copy.27
  41.3 1.3 convolution_add_fusion.23
  42.6 1.2 convolution_add_fusion.22
  45.8 4.3 %collective-permute-start.2 = (bf16[1,16,16,128]{3,2,1,0:T(8,128)(2,1)S(1)}, bf16[1,16,16,128]{3,2,1,0:T(8,128)(2,1)S(1)}, u32[]{:S(2)}, u32[]{:S(2)}) collective-permute-start(bf16[1,16,16,128]{3,2,1,0:T(8,128)(2,1)S(1)} %get-tuple-element.110), channel_id=1, source_target_pairs={{0,1},{1,2},{2,3},{3,4},{4,5},{5,6},{6,7},{7,8},{8,9},{9,10},{10,1... | collective-permute-start | bytes 196616 | tf_op jit(solution)/shard_map/ppermute | solution.py:14
  50.1 1.3 collective-permute-start.3
  58.5 1.2 copy-done.8
  60.8 1.1 fusion.51
  61.9 0.9 copy.35
  62.9 1.0 pad_maximum_fusion.19
  63.8 0.9 copy.43
  64.8 1.0 copy.41
  65.8 0.9 copy.40
  66.8 0.9 copy.38
  67.8 0.9 copy.37
  68.8 2.1 %fusion.39 = (bf16[2,16,16,384]{3,2,1,0:T(8,128)(2,1)S(1)}, bf16[2,16,16,384]{3,2,1,0:T(8,128)(2,1)S(1)}, bf16[2,16,16,384]{3,2,1,0:T(8,128)(2,1)}) fusion(bf16[1,16,16,128]{3,2,1,0:T(8,128)(2,1)} %copy-done.69, bf16[2,16,16,128]{3,2,1,0:T(8,128)(2,1)S(1)} %multiply_convert_fusion, bf16[2,16,16,128]{3,2,1,0:T(8,128)(2,1)} %get-tuple-element.56, ...), kind=kLoop, calls=%fused_computation.93 | loop fusion | flops 4325376 | bytes 2228224 | tf_op jit(solution)/shard_map/concatenate | solution.py:32
  70.9 1.0 copy.42
  71.9 0.9 copy.39
  72.8 1.9 copy.36
  74.8 1.3 fusion.11
  76.1 1.3 fusion.10
  77.5 1.3 fusion.9
  80.5 1.2 copy-done.9
  84.9 0.9 fusion.2
  85.8 38.6 %reduce-scatter.3.cloned.1.call-done = f32[8,3,3,3,128]{4,0,3,2,1:T(8,128)} async-done(((f32[128,3,3,3,128]{4,0,3,2,1:T(8,128)}), f32[8,3,3,3,128]{4,0,3,2,1:T(8,128)}) %reduce-scatter.3.cloned.1.call-update) | async-done | bytes 110608 | tf_op jit(solution)/shard_map/reduce_scatter | solution.py:92
  124.4 62.3 %reduce-scatter.5.cloned.1.call-done = f32[8,3,3,3,128]{4,0,3,2,1:T(8,128)} async-done(((f32[128,3,3,3,128]{4,0,3,2,1:T(8,128)}), f32[8,3,3,3,128]{4,0,3,2,1:T(8,128)}) %reduce-scatter.5.cloned.1.call-update) | async-done | bytes 110608 | tf_op jit(solution)/shard_map/reduce_scatter | solution.py:91
  (212 shorter events, 15.3 us)
Async XLA Ops:
  7.2 117.2 %reduce-scatter.3.cloned.1.call-start = ((), (), s32[]{:S(2)}) async-start(), calls=%async_computation.2 | async-start | bytes 1880064 | tf_op jit(solution)/shard_map/reduce_scatter | solution.py:92
  8.1 18.0 %collective-permute-start = (bf16[1,16,16,128]{3,2,1,0:T(8,128)(2,1)S(1)}, bf16[1,16,16,128]{3,2,1,0:T(8,128)(2,1)S(1)}, u32[]{:S(2)}, u32[]{:S(2)}) collective-permute-start(bf16[1,16,16,128]{3,2,1,0:T(8,128)(2,1)S(1)} %get-tuple-element.115), channel_id=1, source_target_pairs={{0,1},{1,2},{2,3},{3,4},{4,5},{5,6},{6,7},{7,8},{8,9},{9,10},{10,1... | collective-permute-start | bytes 196616 | tf_op jit(solution)/shard_map/ppermute | solution.py:14
  10.5 15.6 %collective-permute-start.1 = (bf16[1,16,16,128]{3,2,1,0:T(8,128)(2,1)S(1)}, bf16[1,16,16,128]{3,2,1,0:T(8,128)(2,1)S(1)}, u32[]{:S(2)}, u32[]{:S(2)}) collective-permute-start(bf16[1,16,16,128]{3,2,1,0:T(8,128)(2,1)S(1)} %get-tuple-element.116), channel_id=1, source_target_pairs={{1,0},{2,1},{3,2},{4,3},{5,4},{6,5},{7,6},{8,7},{9,8},{10,9},{11,1... | collective-permute-start | bytes 196616 | tf_op jit(solution)/shard_map/ppermute | solution.py:15
  12.7 10.9 %collective-permute-start.4 = (bf16[1,16,16,128]{3,2,1,0:T(8,128)(2,1)S(1)}, bf16[1,16,16,128]{3,2,1,0:T(8,128)(2,1)S(1)}, u32[]{:S(2)}, u32[]{:S(2)}) collective-permute-start(bf16[1,16,16,128]{3,2,1,0:T(8,128)(2,1)S(1)} %get-tuple-element.105), channel_id=1, source_target_pairs={{0,1},{1,2},{2,3},{3,4},{4,5},{5,6},{6,7},{7,8},{8,9},{9,10},{10,1... | collective-permute-start | bytes 196616 | tf_op jit(solution)/shard_map/ppermute | solution.py:14
  17.9 5.7 %collective-permute-start.5 = (bf16[1,16,16,128]{3,2,1,0:T(8,128)(2,1)S(1)}, bf16[1,16,16,128]{3,2,1,0:T(8,128)(2,1)S(1)}, u32[]{:S(2)}, u32[]{:S(2)}) collective-permute-start(bf16[1,16,16,128]{3,2,1,0:T(8,128)(2,1)S(1)} %get-tuple-element.106), channel_id=1, source_target_pairs={{1,0},{2,1},{3,2},{4,3},{5,4},{6,5},{7,6},{8,7},{9,8},{10,9},{11,1... | collective-permute-start | bytes 196616 | tf_op jit(solution)/shard_map/ppermute | solution.py:15
  21.2 1.5 copy-start.26
  21.2 2.3 %copy-start = (bf16[2,16,16,128]{3,2,1,0:T(8,128)(2,1)S(1)}, bf16[2,16,16,128]{3,2,1,0:T(8,128)(2,1)}, u32[]{:S(2)}) copy-start(bf16[2,16,16,128]{3,2,1,0:T(8,128)(2,1)} %param.7) | copy-start | bytes 393220
  23.6 1.6 copy-start.64
  23.6 1.6 copy-start.66
  23.8 2.4 %copy-start.25 = (bf16[2,16,16,128]{3,2,1,0:T(8,128)(2,1)S(1)}, bf16[2,16,16,128]{3,2,1,0:T(8,128)(2,1)}, u32[]{:S(2)}) copy-start(bf16[2,16,16,128]{3,2,1,0:T(8,128)(2,1)} %param.4) | copy-start | bytes 393220
  26.1 2.2 %copy-start.70 = (bf16[1,16,16,128]{3,2,1,0:T(8,128)(2,1)}, bf16[1,16,16,128]{3,2,1,0:T(8,128)(2,1)S(1)}, u32[]{:S(2)}) copy-start(bf16[1,16,16,128]{3,2,1,0:T(8,128)(2,1)S(1)} %collective-permute-done) | copy-start | bytes 196612
  26.1 2.2 %copy-start.71 = (bf16[1,16,16,128]{3,2,1,0:T(8,128)(2,1)}, bf16[1,16,16,128]{3,2,1,0:T(8,128)(2,1)S(1)}, u32[]{:S(2)}) copy-start(bf16[1,16,16,128]{3,2,1,0:T(8,128)(2,1)S(1)} %collective-permute-done.1) | copy-start | bytes 196612
  38.5 1.9 copy-start.7
  39.4 4.4 %copy-start.63 = (bf16[1,1,3,128,128]{4,3,2,1,0:T(8,128)(2,1)S(1)}, bf16[1,1,3,128,128]{4,3,2,1,0:T(8,128)(2,1)}, u32[]{:S(2)}) copy-start(bf16[1,1,3,128,128]{4,3,2,1,0:T(8,128)(2,1)} %get-tuple-element.25) | copy-start | bytes 294916
  41.3 2.8 %copy-start.62 = (bf16[1,1,3,128,128]{4,3,2,1,0:T(8,128)(2,1)S(1)}, bf16[1,1,3,128,128]{4,3,2,1,0:T(8,128)(2,1)}, u32[]{:S(2)}) copy-start(bf16[1,1,3,128,128]{4,3,2,1,0:T(8,128)(2,1)} %get-tuple-element.24) | copy-start | bytes 294916
  42.6 1.8 copy-start.61
  44.7 6.7 %copy-start.43 = (bf16[2,16,16,128]{3,2,1,0:T(8,128)(2,1)S(1)}, bf16[2,16,16,128]{3,2,1,0:T(8,128)(2,1)}, u32[]{:S(2)}) copy-start(bf16[2,16,16,128]{3,2,1,0:T(8,128)(2,1)} %get-tuple-element.30) | copy-start | bytes 393220
  44.7 6.7 %copy-start.44 = (bf16[2,16,16,128]{3,2,1,0:T(8,128)(2,1)S(1)}, bf16[2,16,16,128]{3,2,1,0:T(8,128)(2,1)}, u32[]{:S(2)}) copy-start(bf16[2,16,16,128]{3,2,1,0:T(8,128)(2,1)} %get-tuple-element.31) | copy-start | bytes 393220
  44.8 6.7 %copy-start.46 = (bf16[2,16,16,128]{3,2,1,0:T(8,128)(2,1)S(1)}, bf16[2,16,16,128]{3,2,1,0:T(8,128)(2,1)}, u32[]{:S(2)}) copy-start(bf16[2,16,16,128]{3,2,1,0:T(8,128)(2,1)} %get-tuple-element.49) | copy-start | bytes 393220
  44.8 6.7 %copy-start.47 = (bf16[2,16,16,128]{3,2,1,0:T(8,128)(2,1)S(1)}, bf16[2,16,16,128]{3,2,1,0:T(8,128)(2,1)}, u32[]{:S(2)}) copy-start(bf16[2,16,16,128]{3,2,1,0:T(8,128)(2,1)} %get-tuple-element.51) | copy-start | bytes 393220
  44.8 6.7 %copy-start.48 = (bf16[2,16,16,128]{3,2,1,0:T(8,128)(2,1)S(1)}, bf16[2,16,16,128]{3,2,1,0:T(8,128)(2,1)}, u32[]{:S(2)}) copy-start(bf16[2,16,16,128]{3,2,1,0:T(8,128)(2,1)} %get-tuple-element.52) | copy-start | bytes 393220
  44.8 6.7 %copy-start.49 = (bf16[2,16,16,128]{3,2,1,0:T(8,128)(2,1)S(1)}, bf16[2,16,16,128]{3,2,1,0:T(8,128)(2,1)}, u32[]{:S(2)}) copy-start(bf16[2,16,16,128]{3,2,1,0:T(8,128)(2,1)} %get-tuple-element.53) | copy-start | bytes 393220
  45.3 6.2 %copy-start.50 = (bf16[1,1,3,128,128]{4,3,2,1,0:T(8,128)(2,1)S(1)}, bf16[1,1,3,128,128]{4,3,2,1,0:T(8,128)(2,1)}, u32[]{:S(2)}) copy-start(bf16[1,1,3,128,128]{4,3,2,1,0:T(8,128)(2,1)} %get-tuple-element.11) | copy-start | bytes 294916
  45.4 6.6 %copy-start.38 = (bf16[2,16,16,128]{3,2,1,0:T(8,128)(2,1)S(1)}, bf16[2,16,16,128]{3,2,1,0:T(8,128)(2,1)}, u32[]{:S(2)}) copy-start(bf16[2,16,16,128]{3,2,1,0:T(8,128)(2,1)} %get-tuple-element.32) | copy-start | bytes 393220
  45.4 6.6 %copy-start.39 = (bf16[2,16,16,128]{3,2,1,0:T(8,128)(2,1)S(1)}, bf16[2,16,16,128]{3,2,1,0:T(8,128)(2,1)}, u32[]{:S(2)}) copy-start(bf16[2,16,16,128]{3,2,1,0:T(8,128)(2,1)} %get-tuple-element.33) | copy-start | bytes 393220
  45.4 6.6 %copy-start.40 = (bf16[2,16,16,128]{3,2,1,0:T(8,128)(2,1)S(1)}, bf16[2,16,16,128]{3,2,1,0:T(8,128)(2,1)}, u32[]{:S(2)}) copy-start(bf16[2,16,16,128]{3,2,1,0:T(8,128)(2,1)} %get-tuple-element.40) | copy-start | bytes 393220
  45.4 6.6 %copy-start.41 = (bf16[2,16,16,128]{3,2,1,0:T(8,128)(2,1)S(1)}, bf16[2,16,16,128]{3,2,1,0:T(8,128)(2,1)}, u32[]{:S(2)}) copy-start(bf16[2,16,16,128]{3,2,1,0:T(8,128)(2,1)} %get-tuple-element.41) | copy-start | bytes 393220
  45.4 6.6 %copy-start.42 = (bf16[2,16,16,128]{3,2,1,0:T(8,128)(2,1)S(1)}, bf16[2,16,16,128]{3,2,1,0:T(8,128)(2,1)}, u32[]{:S(2)}) copy-start(bf16[2,16,16,128]{3,2,1,0:T(8,128)(2,1)} %get-tuple-element.48) | copy-start | bytes 393220
  45.4 6.6 %copy-start.45 = (bf16[2,16,16,128]{3,2,1,0:T(8,128)(2,1)S(1)}, bf16[2,16,16,128]{3,2,1,0:T(8,128)(2,1)}, u32[]{:S(2)}) copy-start(bf16[2,16,16,128]{3,2,1,0:T(8,128)(2,1)} %get-tuple-element.50) | copy-start | bytes 393220
  45.4 6.6 %copy-start.65 = (bf16[1,16,16,128]{3,2,1,0:T(8,128)(2,1)S(1)}, bf16[1,16,16,128]{3,2,1,0:T(8,128)(2,1)}, u32[]{:S(2)}) copy-start(bf16[1,16,16,128]{3,2,1,0:T(8,128)(2,1)} %copy-done.64) | copy-start | bytes 196612
  45.4 6.6 %copy-start.67 = (bf16[1,16,16,128]{3,2,1,0:T(8,128)(2,1)S(1)}, bf16[1,16,16,128]{3,2,1,0:T(8,128)(2,1)}, u32[]{:S(2)}) copy-start(bf16[1,16,16,128]{3,2,1,0:T(8,128)(2,1)} %copy-done.66) | copy-start | bytes 196612
  45.8 14.2 %collective-permute-start.2 = (bf16[1,16,16,128]{3,2,1,0:T(8,128)(2,1)S(1)}, bf16[1,16,16,128]{3,2,1,0:T(8,128)(2,1)S(1)}, u32[]{:S(2)}, u32[]{:S(2)}) collective-permute-start(bf16[1,16,16,128]{3,2,1,0:T(8,128)(2,1)S(1)} %get-tuple-element.110), channel_id=1, source_target_pairs={{0,1},{1,2},{2,3},{3,4},{4,5},{5,6},{6,7},{7,8},{8,9},{9,10},{10,1... | collective-permute-start | bytes 196616 | tf_op jit(solution)/shard_map/ppermute | solution.py:14
  50.1 9.9 %collective-permute-start.3 = (bf16[1,16,16,128]{3,2,1,0:T(8,128)(2,1)S(1)}, bf16[1,16,16,128]{3,2,1,0:T(8,128)(2,1)S(1)}, u32[]{:S(2)}, u32[]{:S(2)}) collective-permute-start(bf16[1,16,16,128]{3,2,1,0:T(8,128)(2,1)S(1)} %get-tuple-element.111), channel_id=1, source_target_pairs={{1,0},{2,1},{3,2},{4,3},{5,4},{6,5},{7,6},{8,7},{9,8},{10,9},{11,1... | collective-permute-start | bytes 196616 | tf_op jit(solution)/shard_map/ppermute | solution.py:15
  56.0 1.4 copy-start.12
  56.3 1.4 copy-start.11
  56.6 1.4 copy-start.15
  56.9 1.4 copy-start.10
  59.8 127.0 %reduce-scatter.5.cloned.1.call-start = ((), (), s32[]{:S(2)}) async-start(), calls=%async_computation.3 | async-start | bytes 1880064 | tf_op jit(solution)/shard_map/reduce_scatter | solution.py:91
  70.9 6.6 %copy-start.2 = (bf16[2,16,16,384]{3,2,1,0:T(8,128)(2,1)}, bf16[2,16,16,384]{3,2,1,0:T(8,128)(2,1)S(1)}, u32[]{:S(2)}) copy-start(bf16[2,16,16,384]{3,2,1,0:T(8,128)(2,1)S(1)} %get-tuple-element.107) | copy-start | bytes 1179652
  70.9 6.6 %copy-start.4 = (bf16[2,16,16,384]{3,2,1,0:T(8,128)(2,1)}, bf16[2,16,16,384]{3,2,1,0:T(8,128)(2,1)S(1)}, u32[]{:S(2)}) copy-start(bf16[2,16,16,384]{3,2,1,0:T(8,128)(2,1)S(1)} %get-tuple-element.108) | copy-start | bytes 1179652
  74.8 4.1 %copy-start.22 = (bf16[512,384]{0,1:T(8,128)(2,1)S(1)}, bf16[512,384]{0,1:T(8,128)(2,1)}, u32[]{:S(2)}) copy-start(bf16[512,384]{0,1:T(8,128)(2,1)} %copy.38) | copy-start | bytes 1179652
  74.8 4.3 %copy-start.24 = (bf16[512,384]{0,1:T(8,128)(2,1)S(1)}, bf16[512,384]{0,1:T(8,128)(2,1)}, u32[]{:S(2)}) copy-start(bf16[512,384]{0,1:T(8,128)(2,1)} %copy.39) | copy-start | bytes 1179652
  74.8 4.6 %copy-start.21 = (bf16[512,384]{0,1:T(8,128)(2,1)S(1)}, bf16[512,384]{0,1:T(8,128)(2,1)}, u32[]{:S(2)}) copy-start(bf16[512,384]{0,1:T(8,128)(2,1)} %copy.40) | copy-start | bytes 1179652
  76.1 3.5 %copy-start.20 = (bf16[512,384]{0,1:T(8,128)(2,1)S(1)}, bf16[512,384]{0,1:T(8,128)(2,1)}, u32[]{:S(2)}) copy-start(bf16[512,384]{0,1:T(8,128)(2,1)} %copy.41) | copy-start | bytes 1179652
  77.5 2.5 %copy-start.23 = (bf16[512,384]{0,1:T(8,128)(2,1)S(1)}, bf16[512,384]{0,1:T(8,128)(2,1)}, u32[]{:S(2)}) copy-start(bf16[512,384]{0,1:T(8,128)(2,1)} %copy.42) | copy-start | bytes 1179652
  78.8 1.4 copy-start.19
  79.9 1.8 copy-start.1
  81.9 1.7 copy-start.5
  (33 other events, 33.8 us)
Sparse Core Ops, SparseCore 0:
  59.9 64.4 reduce-scatter.2
  128.7 57.9 reduce-scatter.4
where the time goes:
time: 194 us
  waiting for transfers between devices  101 us (52%)
  local copies, waits for them, and re-layouts  35.1 us (18%)
  matrix products  19.2 us (10%)
  starting transfers between devices  16 us (8%)
  between operations  15.4 us (8%)
  other arithmetic  6.97 us (4%)
    reduce_scatter x1, waiting for transfers between devices, per_device(): lax.psum_scatter(second_local, 'space', scatter_dimension=0, tiled=True)  62.3 us
    reduce_scatter x1, waiting for transfers between devices, per_device(): lax.psum_scatter(first_local, 'space', scatter_dimension=0, tiled=True)  38.6 us
    reshape x18, local copies, waits for them, and re-layouts, convolve(): slab.reshape(-1, 3 * inner)  18.1 us
    ppermute x3, starting transfers between devices, padded_2(): before = lax.ppermute(last, axis, up)  11.8 us
    dot_general x27, matrix products, convolve(): jnp.dot(slab.reshape(-1, 3 * inner), weight[plane, column].reshape(3 * in...  11.3 us
    dot_general x18, matrix products, weight_term(): lax.dot_general(slab.reshape(-1, 3 * count), flat, (((0,), (0,)), ((), ()...  7.87 us
    unnamed x147, local copies, waits for them, and re-layouts  7.67 us
    concatenate x15, other arithmetic, convolve(): jnp.concatenate([padded[plane:plane + depth, column:column + width, lane:...  6.39 us
  transfers between devices with their start and end apart: 8, of which 2 were waited for; matrix products, arithmetic and copies ran while one was open for 18% of the time, Pallas kernels for 0%

commit v1 on v0

v1 whole, which is shorter than its diff:
```python
import functools

import jax
import jax.numpy as jnp
from jax import lax
from jax.experimental import pallas as pl
from jax.experimental.pallas import tpu as pltpu
from jax.sharding import PartitionSpec as P

F32, BF16 = jnp.float32, jnp.bfloat16


def gather_taps(x_ref, plane, value, height, reverse=False):
    rows, chans = value.shape
    wide = value.astype(F32)
    lane = lax.rem(lax.broadcasted_iota(jnp.int32, (rows, chans), 0), height)
    before = jnp.where(lane == 0, 0.0, pltpu.roll(wide, 1, 0))
    after = jnp.where(lane == height - 1, 0.0, pltpu.roll(wide, rows - 1, 0))
    edge = jnp.zeros((height, chans), BF16)
    for c, shifted in enumerate((before.astype(BF16), value, after.astype(BF16))):
        for b in range(3):
            tap = b * 3 + c
            tap = 8 - tap if reverse else tap
            cols = slice(tap * chans, (tap + 1) * chans)
            if b == 1:
                x_ref[plane, :, cols] = shifted
            elif b == 0:
                x_ref[plane, :height, cols] = edge
                x_ref[plane, height:, cols] = shifted[: rows - height]
            else:
                x_ref[plane, : rows - height, cols] = shifted[height:]
                x_ref[plane, rows - height :, cols] = edge


def kernel(
    n, depth, height,
    v_ref, w1_ref, w2_ref, c_ref,
    resp_ref, g1_ref, g2_ref,
    xv, xc, xa, w2t, halo, act, hid, agr,
    part, b1, r1, b2, r2, b3, r3,
    hs, hr, s1, q1, s2, q2, s3, q3,
):
    chans = v_ref.shape[1]
    rows = v_ref.shape[0] // depth
    groups = n // 4
    share = chans // n
    me = lax.axis_index("space")
    core = lax.rem(me, 2)
    side = lax.rem(me // 2, 2)
    zme = me // 4
    mate = me + 1 - 2 * core
    across = me + 2 - 4 * side

    barrier = pltpu.get_barrier_semaphore()

    def greet(target):
        pl.semaphore_signal(
            barrier, inc=1, device_id={"space": target}, device_id_type=pl.DeviceIdType.MESH
        )

    def peer(j):
        return lax.rem(zme + j, groups)

    greet(lax.rem(me + 1, n))
    greet(lax.rem(me + n - 1, n))
    greet(across)
    for j in range(1, groups):
        greet(peer(j) * 4 + lax.rem(me, 4))

    def remote(src, dst, send, recv, target):
        return pltpu.make_async_remote_copy(
            src_ref=src, dst_ref=dst, send_sem=send, recv_sem=recv,
            device_id={"space": target}, device_id_type=pl.DeviceIdType.MESH,
        )

    def rims(k, src):
        up = remote(
            src.at[pl.ds((depth - 1) * rows, rows)], halo.at[k, 0], hs.at[k, 0], hr.at[k, 0],
            lax.rem(me + 1, n),
        )
        down = remote(
            src.at[pl.ds(0, rows)], halo.at[k, 1], hs.at[k, 1], hr.at[k, 1],
            lax.rem(me + n - 1, n),
        )
        return up, down

    def send_rims(k, src):
        up, down = rims(k, src)

        @pl.when(me < n - 1)
        def _():
            up.start()

        @pl.when(me > 0)
        def _():
            down.start()

    def take_rims(k, src):
        up, down = rims(k, src)

        @pl.when(me > 0)
        def _():
            up.wait_recv()
            down.wait_send()

        @pl.when(me < n - 1)
        def _():
            down.wait_recv()
            up.wait_send()

    def stretch(x_ref, a):
        return x_ref[a : a + depth].reshape(depth * rows, 9 * chans)

    def own_planes(x_ref, src, reverse=False):
        for p in range(depth):
            gather_taps(x_ref, p + 1, src[p * rows : (p + 1) * rows, :], height, reverse)

    def rim_planes(x_ref, k, reverse=False):
        gather_taps(x_ref, 0, halo[k, 0], height, reverse)
        gather_taps(x_ref, depth + 1, halo[k, 1], height, reverse)

    def mul(x, w):
        return jnp.dot(x, w, preferred_element_type=F32)

    @pl.when(me == 0)
    def _():
        for k in range(3):
            halo[k, 0] = jnp.zeros((rows, chans), BF16)

    @pl.when(me == n - 1)
    def _():
        for k in range(3):
            halo[k, 1] = jnp.zeros((rows, chans), BF16)

    own_planes(xv, v_ref)

    pl.semaphore_wait(barrier, 3 + groups - 1)

    send_rims(0, v_ref)
    send_rims(1, c_ref)
    hid[...] = mul(stretch(xv, 1), w1_ref[1])
    for t in range(27):
        w2t[t // 9, (t % 9) * chans : (t % 9 + 1) * chans, :] = w2_ref[t].T
    own_planes(xc, c_ref, True)
    agr[...] = mul(stretch(xc, 1), w2t[1])

    take_rims(0, v_ref)
    rim_planes(xv, 0)
    hid[...] += mul(stretch(xv, 0), w1_ref[0])
    hid[...] += mul(stretch(xv, 2), w1_ref[2])
    h = hid[...]
    act[...] = (h * jax.nn.sigmoid(h)).astype(BF16)
    send_rims(2, act)

    take_rims(1, c_ref)
    rim_planes(xc, 1, True)
    agr[...] += mul(stretch(xc, 0), w2t[2])
    agr[...] += mul(stretch(xc, 2), w2t[0])
    h = hid[...]
    s = jax.nn.sigmoid(h)
    hgrad = (agr[...] * s * (1.0 + h * (1.0 - s))).astype(BF16)

    def weight_part(k, x_ref, grads):
        for a in range(3):
            term = lax.dot_general(
                stretch(x_ref, a), grads, (((0,), (0,)), ((), ())), preferred_element_type=F32
            )
            for t in range(9):
                part[k, :, :, a * 9 + t] = term[t * chans : (t + 1) * chans].reshape(
                    n // 2, 2, share, chans
                )

    def first_hop(k):
        return remote(b1.at[k], r1.at[k], s1.at[k], q1.at[k], mate)

    def second_hop(k):
        return remote(b2.at[k], r2.at[k], s2.at[k], q2.at[k], across)

    def last_hop(k, j):
        return remote(
            b3.at[k, peer(j)], r3.at[k, zme], s3.at[k, peer(j)], q3.at[k, zme],
            peer(j) * 4 + lax.rem(me, 4),
        )

    def last_in(k, j):
        return remote(
            b3.at[k, peer(j)], r3.at[k, peer(j)], s3.at[k, peer(j)], q3.at[k, peer(j)],
            peer(j) * 4 + lax.rem(me, 4),
        )

    def go_first(k):
        def step(i, _):
            b1[k, i] = part[k, i, 1 - core].astype(BF16)
            return 0

        lax.fori_loop(0, n // 2, step, 0)
        first_hop(k).start()

    def go_second(k):
        first_hop(k).wait()

        def step(z, _):
            i = 2 * z + 1 - side
            b2[k, z] = (part[k, i, core] + r1[k, i].astype(F32)).astype(BF16)
            return 0

        lax.fori_loop(0, groups, step, 0)
        second_hop(k).start()

    def total(k, z):
        i = 2 * z + side
        return part[k, i, core] + r1[k, i].astype(F32) + r2[k, z].astype(F32)

    def go_last(k):
        second_hop(k).wait()
        for j in range(1, groups):
            b3[k, peer(j)] = total(k, peer(j)).astype(BF16)
            last_hop(k, j).start()

    def finish(k, out):
        whole = total(k, zme)
        for j in range(1, groups):
            last_in(k, j).wait_recv()
            whole = whole + r3[k, peer(j)].astype(F32)
        out[...] = whole
        for j in range(1, groups):
            last_hop(k, j).wait_send()

    weight_part(0, xv, hgrad)
    go_first(0)

    own_planes(xa, act)
    take_rims(2, act)
    rim_planes(xa, 2)
    go_second(0)
    weight_part(1, xa, c_ref[...])
    go_first(1)
    go_last(0)
    answer = mul(stretch(xa, 0), w2_ref[0:9].reshape(9 * chans, chans))
    answer += mul(stretch(xa, 1), w2_ref[9:18].reshape(9 * chans, chans))
    answer += mul(stretch(xa, 2), w2_ref[18:27].reshape(9 * chans, chans))
    resp_ref[...] = answer.astype(BF16)
    go_second(1)
    go_last(1)
    finish(0, g1_ref)
    finish(1, g2_ref)


def per_device(n, volume, first_filter, second_filter, cotangent):
    depth, width, height, chans = volume.shape
    rows = width * height
    share = chans // n
    groups = n // 4
    dma = pltpu.SemaphoreType.DMA
    vmem = pl.BlockSpec(memory_space=pltpu.VMEM)
    block = (27, share, chans)
    response, first, second = pl.pallas_call(
        functools.partial(kernel, n, depth, height),
        out_shape=(
            jax.ShapeDtypeStruct((depth * rows, chans), BF16),
            jax.ShapeDtypeStruct(block, F32),
            jax.ShapeDtypeStruct(block, F32),
        ),
        in_specs=[vmem] * 4,
        out_specs=(vmem,) * 3,
        scratch_shapes=[
            pltpu.VMEM((depth + 2, rows, 9 * chans), BF16),
            pltpu.VMEM((depth + 2, rows, 9 * chans), BF16),
            pltpu.VMEM((depth + 2, rows, 9 * chans), BF16),
            pltpu.VMEM((3, 9 * chans, chans), BF16),
            pltpu.VMEM((3, 2, rows, chans), BF16),
            pltpu.VMEM((depth * rows, chans), BF16),
            pltpu.VMEM((depth * rows, chans), F32),
            pltpu.VMEM((depth * rows, chans), F32),
            pltpu.VMEM((2, n // 2, 2) + block, F32),
            pltpu.VMEM((2, n // 2) + block, BF16),
            pltpu.VMEM((2, n // 2) + block, BF16),
            pltpu.VMEM((2, groups) + block, BF16),
            pltpu.VMEM((2, groups) + block, BF16),
            pltpu.VMEM((2, groups) + block, BF16),
            pltpu.VMEM((2, groups) + block, BF16),
            dma((3, 2)), dma((3, 2)),
            dma((2,)), dma((2,)), dma((2,)), dma((2,)),
            dma((2, groups)), dma((2, groups)),
        ],
        compiler_params=pltpu.CompilerParams(
            collective_id=0, has_side_effects=True, vmem_limit_bytes=60 * 1024 * 1024
        ),
    )(
        volume.reshape(depth * rows, chans),
        first_filter.reshape(3, 9 * chans, chans),
        second_filter.reshape(27, chans, chans),
        cotangent.reshape(depth * rows, chans),
    )

    def laid(grad):
        return jnp.transpose(grad, (1, 0, 2)).reshape(share, 3, 3, 3, chans)

    return response.reshape(volume.shape), laid(first), laid(second)


def solution(mesh):
    n = mesh.shape["space"]
    field = P(("parts", "space"), None, None, None)
    grad = P(("parts", "space"), None, None, None, None)
    return jax.shard_map(
        functools.partial(per_device, n),
        mesh=mesh,
        in_specs=(field, P(), P(), field),
        out_specs=(field, grad, grad),
        check_vma=False,
    )
```

time: 194 us -> 39.4 us (0.20)
  waiting for transfers between devices: 101 us -> 0 us
  Pallas kernels: 0 us -> 35.4 us
  local copies, waits for them, and re-layouts: 35.1 us -> 3.19 us
  matrix products: 19.2 us -> 0 us
  starting transfers between devices: 16 us -> 0 us
  between operations: 15.4 us -> 0.65 us
  other arithmetic: 6.97 us -> 0 us
    reduce_scatter x2 -> x0, waiting for transfers between devices: 101 us -> none  [the longest x1 62.3 us: per_device(): lax.psum_scatter(second_local, 'space', scatter_dimension=0, tiled=True)]
    pallas_call x0 -> x1, Pallas kernels: none -> 35.4 us  [per_device(): pl.pallas_call(functools.partial(kernel, n, depth, height), out_shape=(ja...]
    dot_general x45 -> x0, matrix products: 19.2 us -> none  [the longest x27 11.3 us: convolve(): jnp.dot(slab.reshape(-1, 3 * inner), weight[plane, column].reshape(3 * in...]
    reshape x18 -> x0, local copies, waits for them, and re-layouts: 18.1 us -> none  [convolve(): slab.reshape(-1, 3 * inner)]
    ppermute x6 -> x0, starting transfers between devices: 15.7 us -> none  [the longest x3 11.8 us: padded_2(): before = lax.ppermute(last, axis, up)]
    slice x12 -> x0, local copies, waits for them, and re-layouts: 9.26 us -> none  [the longest x6 5.51 us: convolve(): padded[plane:plane + depth, column:column + width, lane:lane + height, :]]
    concatenate x18 -> x0, other arithmetic: 6.89 us -> none  [the longest x15 6.39 us: convolve(): jnp.concatenate([padded[plane:plane + depth, column:column + width, lane:...]
    unnamed x147 -> x7, local copies, waits for them, and re-layouts: 7.67 us -> 3.19 us
  transfers between devices with their start and end apart: 8 -> 0, of which waited for: 2 -> 0; matrix products, arithmetic and copies ran while one was open for 18% -> 0% of each run, Pallas kernels for 0% -> 0%
where the time goes in v1:
time: 39.4 us; the launch traced here: 39.2 us
  Pallas kernels  35.4 us (90%)
  local copies, waits for them, and re-layouts  3.19 us (8%)
  between operations  0.65 us (2%)
    pallas_call x1, Pallas kernels, per_device(): pl.pallas_call(functools.partial(kernel, n, depth, height), out_shape=(ja...  35.4 us
    unnamed x7, local copies, waits for them, and re-layouts  3.19 us

profile of v1, /device:TPU:0, one launch (start us, length us, event | category | flops | bytes accessed | tf_op | source)
XLA Modules:
  0.0 39.2 jit_solution(8981395087990337103)
XLA Ops:
  0.6 35.4 %shard_map.67 = (bf16[512,128]{1,0:T(8,128)(2,1)}, f32[27,8,128]{2,1,0:T(8,128)}, f32[27,8,128]{2,1,0:T(8,128)}) custom-call(bf16[512,128]{1,0:T(8,128)(2,1)} %bitcast.13, bf16[3,1152,128]{2,1,0:T(8,128)(2,1)} %bitcast.11, bf16[27,128,128]{2,1,0:T(8,128)(2,1)} %bitcast.12, bf16[512,128]{1,0:T(8,128)(2,1)} %bitcast.14), custom_call_target="tpu_custom_call" | custom-call | tf_op jit(solution)/shard_map/pallas_call | solution.py:257
  36.0 0.0 copy-start.1
  36.1 1.6 %copy.10 = bf16[2,16,16,128]{3,2,1,0:T(8,128)(2,1)} copy(bf16[2,16,16,128]{3,2,1,0:T(8,128)(2,1)} %bitcast.15) | data formatting | bytes 262144
  37.7 0.0 copy-done.1
  37.7 0.0 copy-start
  37.7 0.6 %copy.11 = f32[8,3,3,3,128]{4,0,3,2,1:T(8,128)} copy(f32[8,3,3,3,128]{4,0,3,2,1:T(8,128)S(1)} %bitcast.17) | data formatting | bytes 221184
  38.3 0.3 copy-done
  38.6 0.6 %copy.12 = f32[8,3,3,3,128]{4,0,3,2,1:T(8,128)} copy(f32[8,3,3,3,128]{4,0,3,2,1:T(8,128)S(1)} %bitcast.16) | data formatting | bytes 221184
Async XLA Ops:
  36.0 1.6 %copy-start.1 = (f32[27,8,128]{2,1,0:T(8,128)S(1)}, f32[27,8,128]{2,1,0:T(8,128)}, u32[]{:S(2)}) copy-start(f32[27,8,128]{2,1,0:T(8,128)} %get-tuple-element.7) | copy-start | bytes 331780
  37.7 0.9 %copy-start = (f32[27,8,128]{2,1,0:T(8,128)S(1)}, f32[27,8,128]{2,1,0:T(8,128)}, u32[]{:S(2)}) copy-start(f32[27,8,128]{2,1,0:T(8,128)} %get-tuple-element.8) | copy-start | bytes 331780

commit v2 on v1

--- a/solution.py
+++ b/solution.py
@@ -34,8 +34,9 @@
 
 def kernel(
     n, depth, height,
-    v_ref, w1_ref, w2_ref, c_ref,
-    resp_ref, g1_ref, g2_ref,
+    v_hbm, w1_hbm, w2_hbm, c_hbm,
+    resp_hbm, g1_hbm, g2_hbm,
+    v_ref, w1_ref, w2_ref, c_ref, resp_ref, sums, ins, outs,
     xv, xc, xa, w2t, halo, act, hid, agr,
     part, b1, r1, b2, r2, b3, r3,
     hs, hr, s1, q1, s2, q2, s3, q3,
@@ -73,6 +74,21 @@
             device_id={"space": target}, device_id_type=pl.DeviceIdType.MESH,
         )
 
+    def load(i, src, dst):
+        return pltpu.make_async_copy(src, dst, ins.at[i])
+
+    def save(i, src, dst):
+        return pltpu.make_async_copy(src, dst, outs.at[i])
+
+    loads = (
+        load(0, v_hbm, v_ref),
+        load(1, c_hbm, c_ref),
+        load(2, w1_hbm, w1_ref),
+        load(3, w2_hbm, w2_ref),
+    )
+    for copy in loads:
+        copy.start()
+
     def rims(k, src):
         up = remote(
             src.at[pl.ds((depth - 1) * rows, rows)], halo.at[k, 0], hs.at[k, 0], hr.at[k, 0],
@@ -132,13 +148,17 @@
         for k in range(3):
             halo[k, 1] = jnp.zeros((rows, chans), BF16)
 
+    loads[0].wait()
     own_planes(xv, v_ref)
+    loads[1].wait()
 
     pl.semaphore_wait(barrier, 3 + groups - 1)
 
     send_rims(0, v_ref)
     send_rims(1, c_ref)
+    loads[2].wait()
     hid[...] = mul(stretch(xv, 1), w1_ref[1])
+    loads[3].wait()
     for t in range(27):
         w2t[t // 9, (t % 9) * chans : (t % 9 + 1) * chans, :] = w2_ref[t].T
     own_planes(xc, c_ref, True)
@@ -235,15 +255,21 @@
     go_second(0)
     weight_part(1, xa, c_ref[...])
     go_first(1)
-    go_last(0)
+    go_second(1)
     answer = mul(stretch(xa, 0), w2_ref[0:9].reshape(9 * chans, chans))
     answer += mul(stretch(xa, 1), w2_ref[9:18].reshape(9 * chans, chans))
     answer += mul(stretch(xa, 2), w2_ref[18:27].reshape(9 * chans, chans))
     resp_ref[...] = answer.astype(BF16)
-    go_second(1)
+    save(2, resp_ref, resp_hbm).start()
+    go_last(0)
     go_last(1)
-    finish(0, g1_ref)
-    finish(1, g2_ref)
+    finish(0, sums.at[0])
+    save(0, sums.at[0], g1_hbm).start()
+    finish(1, sums.at[1])
+    save(1, sums.at[1], g2_hbm).start()
+    save(2, resp_ref, resp_hbm).wait()
+    save(0, sums.at[0], g1_hbm).wait()
+    save(1, sums.at[1], g2_hbm).wait()
 
 
 def per_device(n, volume, first_filter, second_filter, cotangent):
@@ -252,7 +278,7 @@
     share = chans // n
     groups = n // 4
     dma = pltpu.SemaphoreType.DMA
-    vmem = pl.BlockSpec(memory_space=pltpu.VMEM)
+    hbm = pl.BlockSpec(memory_space=pl.ANY)
     block = (27, share, chans)
     response, first, second = pl.pallas_call(
         functools.partial(kernel, n, depth, height),
@@ -261,9 +287,16 @@
             jax.ShapeDtypeStruct(block, F32),
             jax.ShapeDtypeStruct(block, F32),
         ),
-        in_specs=[vmem] * 4,
-        out_specs=(vmem,) * 3,
+        in_specs=[hbm] * 4,
+        out_specs=(hbm,) * 3,
         scratch_shapes=[
+            pltpu.VMEM((depth * rows, chans), BF16),
+            pltpu.VMEM((3, 9 * chans, chans), BF16),
+            pltpu.VMEM((27, chans, chans), BF16),
+            pltpu.VMEM((depth * rows, chans), BF16),
+            pltpu.VMEM((depth * rows, chans), BF16),
+            pltpu.VMEM((2,) + block, F32),
+            dma((4,)), dma((3,)),
             pltpu.VMEM((depth + 2, rows, 9 * chans), BF16),
             pltpu.VMEM((depth + 2, rows, 9 * chans), BF16),
             pltpu.VMEM((depth + 2, rows, 9 * chans), BF16),

time: 39.4 us -> 34.6 us (0.88)
  Pallas kernels: 35.4 us -> 30.6 us
    pallas_call x1, Pallas kernels: 35.4 us -> 30.6 us  [per_device(): pl.pallas_call(functools.partial(kernel, n, depth, height), out_shape=(ja...]
where the time goes in v2:
time: 34.6 us; the launch traced here: 34.4 us
  Pallas kernels  30.6 us (88%)
  local copies, waits for them, and re-layouts  3.19 us (9%)
  between operations  0.65 us (2%)
    pallas_call x1, Pallas kernels, per_device(): pl.pallas_call(functools.partial(kernel, n, depth, height), out_shape=(ja...  30.6 us
    unnamed x7, local copies, waits for them, and re-layouts  3.19 us

profile of v2, /device:TPU:0, one launch (start us, length us, event | category | flops | bytes accessed | tf_op | source)
XLA Modules:
  0.0 34.4 jit_solution(15099156656150413998)
XLA Ops:
  0.6 30.6 %shard_map.67 = (bf16[512,128]{1,0:T(8,128)(2,1)}, f32[27,8,128]{2,1,0:T(8,128)}, f32[27,8,128]{2,1,0:T(8,128)}) custom-call(bf16[512,128]{1,0:T(8,128)(2,1)} %bitcast.13, bf16[3,1152,128]{2,1,0:T(8,128)(2,1)} %bitcast.11, bf16[27,128,128]{2,1,0:T(8,128)(2,1)} %bitcast.12, bf16[512,128]{1,0:T(8,128)(2,1)} %bitcast.14), custom_call_target="tpu_custom_call" | custom-call | tf_op jit(solution)/shard_map/pallas_call | solution.py:283
  31.2 0.0 copy-start.1
  31.2 1.6 %copy.10 = bf16[2,16,16,128]{3,2,1,0:T(8,128)(2,1)} copy(bf16[2,16,16,128]{3,2,1,0:T(8,128)(2,1)} %bitcast.15) | data formatting | bytes 262144
  32.8 0.0 copy-done.1
  32.8 0.0 copy-start
  32.8 0.6 %copy.11 = f32[8,3,3,3,128]{4,0,3,2,1:T(8,128)} copy(f32[8,3,3,3,128]{4,0,3,2,1:T(8,128)S(1)} %bitcast.17) | data formatting | bytes 221184
  33.5 0.3 copy-done
  33.8 0.6 %copy.12 = f32[8,3,3,3,128]{4,0,3,2,1:T(8,128)} copy(f32[8,3,3,3,128]{4,0,3,2,1:T(8,128)S(1)} %bitcast.16) | data formatting | bytes 221184
Async XLA Ops:
  31.2 1.6 %copy-start.1 = (f32[27,8,128]{2,1,0:T(8,128)S(1)}, f32[27,8,128]{2,1,0:T(8,128)}, u32[]{:S(2)}) copy-start(f32[27,8,128]{2,1,0:T(8,128)} %get-tuple-element.7) | copy-start | bytes 331780
  32.8 0.9 %copy-start = (f32[27,8,128]{2,1,0:T(8,128)S(1)}, f32[27,8,128]{2,1,0:T(8,128)}, u32[]{:S(2)}) copy-start(f32[27,8,128]{2,1,0:T(8,128)} %get-tuple-element.8) | copy-start | bytes 331780

commit v3 on v2

--- a/solution.py
+++ b/solution.py
@@ -180,15 +180,15 @@
     s = jax.nn.sigmoid(h)
     hgrad = (agr[...] * s * (1.0 + h * (1.0 - s))).astype(BF16)
 
-    def weight_part(k, x_ref, grads):
-        for a in range(3):
-            term = lax.dot_general(
-                stretch(x_ref, a), grads, (((0,), (0,)), ((), ())), preferred_element_type=F32
+    def weight_piece(k, x_ref, grads):
+        term = lax.dot_general(
+            stretch(x_ref, k % 3), grads, (((0,), (0,)), ((), ())), preferred_element_type=F32
+        )
+        for t in range(9):
+            part[k, :, :, t] = term[t * chans : (t + 1) * chans].reshape(
+                n // 2, 2, share, chans
             )
-            for t in range(9):
-                part[k, :, :, a * 9 + t] = term[t * chans : (t + 1) * chans].reshape(
-                    n // 2, 2, share, chans
-                )
+        go_first(k)
 
     def first_hop(k):
         return remote(b1.at[k], r1.at[k], s1.at[k], q1.at[k], mate)
@@ -237,35 +237,44 @@
             b3[k, peer(j)] = total(k, peer(j)).astype(BF16)
             last_hop(k, j).start()
 
-    def finish(k, out):
+    def finish(k):
         whole = total(k, zme)
         for j in range(1, groups):
             last_in(k, j).wait_recv()
             whole = whole + r3[k, peer(j)].astype(F32)
-        out[...] = whole
+        sums[k // 3, 9 * (k % 3) : 9 * (k % 3) + 9] = whole
         for j in range(1, groups):
             last_hop(k, j).wait_send()
 
-    weight_part(0, xv, hgrad)
-    go_first(0)
-
+    weight_piece(0, xv, hgrad)
+    weight_piece(1, xv, hgrad)
+    go_second(0)
+    weight_piece(2, xv, hgrad)
+    go_second(1)
     own_planes(xa, act)
+    go_second(2)
     take_rims(2, act)
     rim_planes(xa, 2)
-    go_second(0)
-    weight_part(1, xa, c_ref[...])
-    go_first(1)
-    go_second(1)
+    weight_piece(3, xa, c_ref[...])
+    weight_piece(4, xa, c_ref[...])
+    go_second(3)
+    go_last(0)
+    weight_piece(5, xa, c_ref[...])
+    go_second(4)
+    go_last(1)
+    go_second(5)
     answer = mul(stretch(xa, 0), w2_ref[0:9].reshape(9 * chans, chans))
     answer += mul(stretch(xa, 1), w2_ref[9:18].reshape(9 * chans, chans))
     answer += mul(stretch(xa, 2), w2_ref[18:27].reshape(9 * chans, chans))
     resp_ref[...] = answer.astype(BF16)
     save(2, resp_ref, resp_hbm).start()
-    go_last(0)
-    go_last(1)
-    finish(0, sums.at[0])
+    for k in range(2, 6):
+        go_last(k)
+    for k in range(3):
+        finish(k)
     save(0, sums.at[0], g1_hbm).start()
-    finish(1, sums.at[1])
+    for k in range(3, 6):
+        finish(k)
     save(1, sums.at[1], g2_hbm).start()
     save(2, resp_ref, resp_hbm).wait()
     save(0, sums.at[0], g1_hbm).wait()
@@ -280,6 +289,7 @@
     dma = pltpu.SemaphoreType.DMA
     hbm = pl.BlockSpec(memory_space=pl.ANY)
     block = (27, share, chans)
+    piece = (9, share, chans)
     response, first, second = pl.pallas_call(
         functools.partial(kernel, n, depth, height),
         out_shape=(
@@ -305,16 +315,16 @@
             pltpu.VMEM((depth * rows, chans), BF16),
             pltpu.VMEM((depth * rows, chans), F32),
             pltpu.VMEM((depth * rows, chans), F32),
-            pltpu.VMEM((2, n // 2, 2) + block, F32),
-            pltpu.VMEM((2, n // 2) + block, BF16),
-            pltpu.VMEM((2, n // 2) + block, BF16),
-            pltpu.VMEM((2, groups) + block, BF16),
-            pltpu.VMEM((2, groups) + block, BF16),
-            pltpu.VMEM((2, groups) + block, BF16),
-            pltpu.VMEM((2, groups) + block, BF16),
+            pltpu.VMEM((6, n // 2, 2) + piece, F32),
+            pltpu.VMEM((6, n // 2) + piece, BF16),
+            pltpu.VMEM((6, n // 2) + piece, BF16),
+            pltpu.VMEM((6, groups) + piece, BF16),
+            pltpu.VMEM((6, groups) + piece, BF16),
+            pltpu.VMEM((6, groups) + piece, BF16),
+            pltpu.VMEM((6, groups) + piece, BF16),
             dma((3, 2)), dma((3, 2)),
-            dma((2,)), dma((2,)), dma((2,)), dma((2,)),
-            dma((2, groups)), dma((2, groups)),
+            dma((6,)), dma((6,)), dma((6,)), dma((6,)),
+            dma((6, groups)), dma((6, groups)),
         ],
         compiler_params=pltpu.CompilerParams(
             collective_id=0, has_side_effects=True, vmem_limit_bytes=60 * 1024 * 1024

time: 34.6 us -> 33.7 us (0.974)
  Pallas kernels: 30.6 us -> 29.7 us
    pallas_call x1, Pallas kernels: 30.6 us -> 29.7 us  [per_device(): pl.pallas_call(functools.partial(kernel, n, depth, height), out_shape=(ja...]
where the time goes in v3:
time: 33.7 us; the launch traced here: 33.5 us
  Pallas kernels  29.7 us (88%)
  local copies, waits for them, and re-layouts  3.19 us (9%)
  between operations  0.65 us (2%)
    pallas_call x1, Pallas kernels, per_device(): pl.pallas_call(functools.partial(kernel, n, depth, height), out_shape=(ja...  29.7 us
    unnamed x7, local copies, waits for them, and re-layouts  3.19 us

profile of v3, /device:TPU:0, one launch (start us, length us, event | category | flops | bytes accessed | tf_op | source)
XLA Modules:
  0.0 33.5 jit_solution(2191925691633135211)
XLA Ops:
  0.6 29.7 %shard_map.67 = (bf16[512,128]{1,0:T(8,128)(2,1)}, f32[27,8,128]{2,1,0:T(8,128)}, f32[27,8,128]{2,1,0:T(8,128)}) custom-call(bf16[512,128]{1,0:T(8,128)(2,1)} %bitcast.13, bf16[3,1152,128]{2,1,0:T(8,128)(2,1)} %bitcast.11, bf16[27,128,128]{2,1,0:T(8,128)(2,1)} %bitcast.12, bf16[512,128]{1,0:T(8,128)(2,1)} %bitcast.14), custom_call_target="tpu_custom_call" | custom-call | tf_op jit(solution)/shard_map/pallas_call | solution.py:293
  30.3 0.0 copy-start.1
  30.3 1.6 %copy.10 = bf16[2,16,16,128]{3,2,1,0:T(8,128)(2,1)} copy(bf16[2,16,16,128]{3,2,1,0:T(8,128)(2,1)} %bitcast.15) | data formatting | bytes 262144
  31.9 0.0 copy-done.1
  31.9 0.0 copy-start
  31.9 0.6 %copy.11 = f32[8,3,3,3,128]{4,0,3,2,1:T(8,128)} copy(f32[8,3,3,3,128]{4,0,3,2,1:T(8,128)S(1)} %bitcast.17) | data formatting | bytes 221184
  32.6 0.3 copy-done
  32.9 0.6 %copy.12 = f32[8,3,3,3,128]{4,0,3,2,1:T(8,128)} copy(f32[8,3,3,3,128]{4,0,3,2,1:T(8,128)S(1)} %bitcast.16) | data formatting | bytes 221184
Async XLA Ops:
  30.3 1.6 %copy-start.1 = (f32[27,8,128]{2,1,0:T(8,128)S(1)}, f32[27,8,128]{2,1,0:T(8,128)}, u32[]{:S(2)}) copy-start(f32[27,8,128]{2,1,0:T(8,128)} %get-tuple-element.7) | copy-start | bytes 331780
  31.9 0.9 %copy-start = (f32[27,8,128]{2,1,0:T(8,128)S(1)}, f32[27,8,128]{2,1,0:T(8,128)}, u32[]{:S(2)}) copy-start(f32[27,8,128]{2,1,0:T(8,128)} %get-tuple-element.8) | copy-start | bytes 331780
